TPU v7x, 32 devices: a whole 2x2x4 slice. The times are simulated.
32 devices in a mesh: dp: 8 (over y, x, core), shard: 4 (over z).
Axes of the slice: x: 2, y: 2, z: 4, core: 2. Of those that a mesh axis runs over, the one named last changes fastest.
Arguments:
- activations: bfloat16 [4096, 4096], P('dp', 'shard'), may hold values from -6 to 6
- out_grads: bfloat16 [4096, 14336], P('dp', 'shard'), may hold values from -6 to 6
- sign_bits: int32 [14336], P('shard'), may hold values from 0 to 1
- block_ids: int32 [4, 8], replicated, may hold values from 0 to 111, as said below
Outputs:
- gram: float32 [4096, 1024], P('shard')
Inputs may be any that keep to these rules, and one draw needn't show every extreme that they name: `block_ids`: row o holds 4 runs of 2 entries; the entries of a run are distinct blocks of one shard s (ids s * 28 + 0 to s * 28 + 27), and the runs of a row come from distinct shards.
All inputs are finite; a program needn't handle non-finite values.
Results may differ from a plain program's by a relative error of at most 0.006.
Values may be sent and summed in bfloat16 or wider, within the bound.
A program may use at most 64 MiB of HBM per device.

v0:
```python
import math

import jax
import jax.numpy as jnp
from jax import lax
from jax.sharding import PartitionSpec as P

BLK = 128
CAP = 2


def partner_2(x, axis, distance):
    return lax.ppermute(x, axis, [(i, i ^ 1 << distance) for i in range(lax.axis_size(axis))])


def parity_table(count):
    index = jnp.arange(count, dtype=jnp.int32)
    total = jnp.zeros((count, count), jnp.int32)
    for level in range(count.bit_length() - 1):
        total = total + (
            jnp.right_shift(index[:, None], level) & jnp.right_shift(index[None, :], level) & 1
        )
    return (1 - 2 * (total % 2)).astype(jnp.float32)


def route_sampled(mixed, block_ids, me_index, shards, blocks_per, tokens, width):
    groups = block_ids.shape[1] // CAP
    sources = block_ids[:, ::CAP] // blocks_per
    local_ids = (block_ids % blocks_per).reshape(shards, groups, CAP)
    matched = sources == me_index
    chosen = jnp.sum(jnp.where(matched[:, :, None], local_ids, 0), axis=1)
    live_rows = jnp.any(matched, axis=1).astype(jnp.bfloat16)
    outgoing = jnp.take(mixed, chosen.reshape(-1), axis=0).reshape(shards, CAP, tokens, width)
    return (outgoing * live_rows[:, None, None, None], jnp.take(sources, me_index, axis=0))


def body(activations, out_grads, sign_bits, block_ids):
    shards = lax.axis_size("shard")
    me_index = lax.axis_index("shard")
    tokens = out_grads.shape[0]
    width = BLK
    own_blocks = block_ids.shape[1]
    blocks_per = out_grads.shape[1] // width
    model_width = activations.shape[1] * shards
    inv_block = 1.0 / math.sqrt(width)
    inv_shard = 1.0 / math.sqrt(shards)
    partial_gram = jnp.dot(activations, activations.T, preferred_element_type=jnp.float32)
    token_gram = lax.psum(partial_gram, "shard").astype(jnp.bfloat16)
    sign_values = (1 - 2 * sign_bits).astype(jnp.bfloat16)
    flipped = (out_grads * sign_values[None, :]).reshape(tokens, blocks_per, width)
    block_table = parity_table(width).astype(jnp.bfloat16)
    local_mix = jnp.einsum("tbj,jk->btk", flipped, block_table, preferred_element_type=jnp.float32)
    local_mix = (local_mix * inv_block).astype(jnp.bfloat16)
    running = local_mix.astype(jnp.float32)
    for level in range(shards.bit_length() - 1):
        partner = partner_2(running, "shard", level)
        upper = jnp.right_shift(me_index, level) & 1 == 1
        running = jnp.where(upper, partner - running, running + partner)
    mixed = (running * inv_shard).astype(jnp.bfloat16)
    outgoing, own_sources = route_sampled(
        mixed, block_ids, me_index, shards, blocks_per, tokens, width
    )
    incoming = lax.all_to_all(outgoing, "shard", split_axis=0, concat_axis=0, tiled=True)
    sketched = jnp.take(incoming, own_sources, axis=0).reshape(own_blocks, tokens, width)
    weighted = jnp.einsum(
        "tu,jub->jtb", token_gram, sketched, preferred_element_type=jnp.float32
    ).astype(jnp.bfloat16)
    block_gram = jnp.einsum("jtb,ktc->jbkc", sketched, weighted, preferred_element_type=jnp.float32)
    own_cols = own_blocks * width
    block_gram = block_gram.reshape(own_cols, own_cols)
    summed = lax.psum(block_gram, "dp")
    return summed / (lax.axis_size("dp") * tokens * model_width)


def solution(mesh):
    in_specs = (P("dp", "shard"), P("dp", "shard"), P("shard"), P())
    out_specs = P("shard", None)
    return jax.shard_map(body, mesh=mesh, in_specs=in_specs, out_specs=out_specs, check_vma=False)
```

profile of v0, /device:TPU:0, one launch (start us, length us, event | category | flops | bytes accessed | tf_op | source)
XLA Modules:
  0.0 690.9 jit_solution(8151458818415333310)
XLA Ops:
  6.5 0.0 copy-start
  6.5 0.0 copy-start.1
  6.6 6.0 copy.15
  12.6 0.0 copy-done.1
  12.6 3.3 broadcast_multiply_fusion.1
  15.9 4.3 convert_bitcast_fusion
  20.2 3.1 collective-permute-start
  23.3 0.0 copy-start.2
  23.3 158.3 %collective-permute-done = f32[28,512,128]{1,2,0:T(8,128)} collective-permute-done((f32[28,512,128]{1,2,0:T(8,128)}, f32[28,512,128]{1,2,0:T(8,128)}, u32[]{:S(2)}, u32[]{:S(2)}) %collective-permute-start) | collective-permute-done | bytes 7340064 | tf_op jit(solution)/shard_map/ppermute | solution.py:13
  181.6 10.6 %add_select_fusion = f32[28,512,128]{1,2,0:T(8,128)} fusion(f32[28,512,128]{1,2,0:T(8,128)} %convert_bitcast_fusion, f32[28,512,128]{1,2,0:T(8,128)} %collective-permute-done, pred[]{:T(512)S(6)} %eq.19), kind=kLoop, calls=%fused_computation.4 | loop fusion | flops 5505024 | bytes 22020096 | tf_op jit(solution)/shard_map/jit(_where)/select_n | solution.py:58
  192.1 2.8 collective-permute-start.1
  194.9 0.0 copy-done.2
  194.9 0.1 slice.3
  195.0 0.1 copy.13
  195.1 0.1 fusion.32
  195.2 0.1 copy.12
  195.3 0.1 copy.17
  195.4 0.1 reshape.154
  195.5 0.1 copy.14
  195.7 0.1 broadcast_in_dim.63
  195.7 0.1 broadcast_in_dim.64
  195.8 314.0 %collective-permute-done.1 = f32[28,512,128]{1,2,0:T(8,128)} collective-permute-done((f32[28,512,128]{1,2,0:T(8,128)}, f32[28,512,128]{1,2,0:T(8,128)}, u32[]{:S(2)}, u32[]{:S(2)}) %collective-permute-start.1) | collective-permute-done | bytes 7340064 | tf_op jit(solution)/shard_map/ppermute | solution.py:13
  509.8 9.1 %multiply_convert_fusion = bf16[28,512,128]{1,2,0:T(8,128)(2,1)} fusion(f32[28,512,128]{1,2,0:T(8,128)} %add_select_fusion, f32[28,512,128]{1,2,0:T(8,128)} %collective-permute-done.1, pred[]{:T(512)S(6)} %eq.18), kind=kLoop, calls=%fused_computation.3 | loop fusion | flops 9175040 | bytes 18350080 | tf_op jit(solution)/shard_map/convert_element_type | solution.py:59
  518.9 2.6 gather_fusion
  521.5 1.1 select_multiply_fusion
  522.7 4.6 all-to-all-start
  527.3 0.0 all-reduce.3.cloned.1.call-start
  527.3 0.0 copy-done
  527.3 0.7 fusion.33
  528.1 63.9 %all-reduce.4 = bf16[512,512]{1,0:T(8,128)(2,1)} all-reduce(f32[512,512]{1,0:T(8,128)S(1)} %fusion.33), channel_id=1, replica_groups=mesh['dp'=8,'shard'=4] {'shard'}, use_global_device_ids=true, to_apply=%region_2.3 | all-reduce | flops 262144 | bytes 1572864 | tf_op jit(solution)/shard_map/psum | solution.py:48
  591.9 0.0 all-to-all-done
  591.9 0.6 gather_fusion.1
  592.6 0.2 bitcast_select_fusion
  592.7 1.8 convolution_convert_fusion
  594.5 3.3 fusion.34
  597.8 0.0 all-reduce.3.cloned.1.call-update
  597.8 81.2 %all-reduce.3.cloned.1.call-done = f32[1024,1024]{1,0:T(8,128)} async-done(((f32[1024,1024]{1,0:T(8,128)}), f32[1024,1024]{1,0:T(8,128)}) %all-reduce.3.cloned.1.call-update) | async-done | bytes 4194320 | tf_op jit(solution)/shard_map/psum | solution.py:71
  679.0 5.0 broadcast_multiply_fusion
  (14 shorter events, 0.1 us)
Async XLA Ops:
  6.5 520.8 %copy-start = (bf16[512,1024]{1,0:T(8,128)(2,1)S(1)}, bf16[512,1024]{1,0:T(8,128)(2,1)}, u32[]{:S(2)}) copy-start(bf16[512,1024]{1,0:T(8,128)(2,1)} %param.4) | copy-start | bytes 3145732
  6.5 6.0 copy-start.1
  20.2 161.4 %collective-permute-start = (f32[28,512,128]{1,2,0:T(8,128)}, f32[28,512,128]{1,2,0:T(8,128)}, u32[]{:S(2)}, u32[]{:S(2)}) collective-permute-start(f32[28,512,128]{1,2,0:T(8,128)} %convert_bitcast_fusion), channel_id=1, source_target_pairs={{0,1},{1,0},{2,3},{3,2},{4,5},{5,4},{6,7},{7,6},{8,9},{9,8},{10,11... | collective-permute-start | bytes 22020104 | tf_op jit(solution)/shard_map/ppermute | solution.py:13
  23.3 171.6 %copy-start.2 = (s32[4,8]{1,0:T(4,128)S(1)}, s32[4,8]{1,0:T(4,128)}, u32[]{:S(2)}) copy-start(s32[4,8]{1,0:T(4,128)} %param.7) | copy-start | bytes 388
  192.1 317.7 %collective-permute-start.1 = (f32[28,512,128]{1,2,0:T(8,128)}, f32[28,512,128]{1,2,0:T(8,128)}, u32[]{:S(2)}, u32[]{:S(2)}) collective-permute-start(f32[28,512,128]{1,2,0:T(8,128)} %add_select_fusion), channel_id=1, source_target_pairs={{0,2},{1,3},{2,0},{3,1},{4,6},{5,7},{6,4},{7,5},{8,10},{9,11},{10,... | collective-permute-start | bytes 22020104 | tf_op jit(solution)/shard_map/ppermute | solution.py:13
  522.7 69.3 %all-to-all-start = ((bf16[4,2,512,128]{2,3,1,0:T(8,128)(2,1)}), bf16[4,2,512,128]{2,3,1,0:T(8,128)(2,1)S(1)}, u32[]{:S(2)}, u32[]{:S(2)}) async-start(bf16[4,2,512,128]{2,3,1,0:T(8,128)(2,1)} %select_multiply_fusion), calls=%async_computation | async-start | bytes 2097152 | tf_op jit(solution)/shard_map/all_to_all | solution.py:63
  527.3 151.7 %all-reduce.3.cloned.1.call-start = ((), (), s32[]{:S(2)}) async-start(), calls=%async_computation.1 | async-start | bytes 8388608 | tf_op jit(solution)/shard_map/psum | solution.py:71
Sparse Core Ops, SparseCore 0:
  598.0 80.9 all-reduce.2
where the time goes:
time: 691 us
  waiting for transfers between devices  553 us (80%)
  blocking collectives  63.9 us (9%)
  other arithmetic  29.5 us (4%)
  between operations  13.5 us (2%)
  starting transfers between devices  10.5 us (2%)
  matrix products  10.1 us (1%)
  local copies, waits for them, and re-layouts  10 us (1%)
    ppermute x2, waiting for transfers between devices, partner_2(): lax.ppermute(x, axis, [(i, i ^ 1 << distance) for i in range(lax.axis_siz...  472 us
    psum x1, waiting for transfers between devices, body(): summed = lax.psum(block_gram, 'dp')  81.2 us
    psum x1, blocking collectives, body(): token_gram = lax.psum(partial_gram, 'shard').astype(jnp.bfloat16)  63.9 us
  transfers between devices with their start and end apart: 4, of which 3 were waited for; matrix products, arithmetic and copies ran while one was open for 0% of the time, Pallas kernels for 0%

commit v1 on v0

--- a/solution.py
+++ b/solution.py
@@ -1,8 +1,11 @@
+import functools
 import math
 
 import jax
 import jax.numpy as jnp
 from jax import lax
+from jax.experimental import pallas as pl
+from jax.experimental.pallas import tpu as pltpu
 from jax.sharding import PartitionSpec as P
 
 BLK = 128
@@ -72,7 +75,440 @@
     return summed / (lax.axis_size("dp") * tokens * model_width)
 
 
+ALONG = pl.DeviceIdType.MESH
+CHUNKS = 4
+GP = ((0, 0), (256, 256), (256, 0))
+FIRST = (0, 1, 3, 6, 10)
+
+
+def pick_kernel(shards, own, per, ids, bits, grads, out, held, i_sem, o_sem):
+    z = lax.axis_index("shard")
+    width = BLK
+    number = shards * own
+
+    def start_of(p):
+        block = ids[p]
+        r = block // per
+        return r, pl.multiple_of((block - r * per) * width, width)
+
+    def fetch(p):
+        return pltpu.make_async_copy(grads.at[:, pl.ds(start_of(p)[1], width)], held.at[p], i_sem.at[p])
+
+    def put(p):
+        return pltpu.make_async_copy(held.at[p], out.at[p], o_sem.at[p])
+
+    def first(p, carry):
+        fetch(p).start()
+        return carry
+
+    def middle(p, carry):
+        r, start = start_of(p)
+        common = r & z
+        odd = common & 1
+        for level in range(1, shards.bit_length() - 1):
+            odd = odd + ((common >> level) & 1)
+        sign = 1 - 2 * (odd & 1)
+        signs = ((1 - 2 * bits[:, pl.ds(start, width)]) * sign).astype(jnp.float32).astype(jnp.bfloat16)
+        fetch(p).wait()
+        held[p] = held[p] * signs
+        put(p).start()
+        return carry
+
+    def end(p, carry):
+        put(p).wait()
+        return carry
+
+    lax.fori_loop(0, number, first, 0)
+    lax.fori_loop(0, number, middle, 0)
+    lax.fori_loop(0, number, end, 0)
+
+
+def mix_kernel(
+    shards, parts, own, act, picked, out,
+    rx, tx, grx, gtx, part, full, sketch, halves, prx, rtx, rrx, gathered,
+    z_send, z_recv, p_send, p_recv, r_send, r_recv, f_send, f_recv, a_send, a_recv, w_send, w_recv,
+):
+    z = lax.axis_index("shard")
+    d = lax.axis_index("dp")
+    core = lax.rem(d, 2)
+    chip = d // 2
+    last = shards - 1
+    edge = (z == 0) | (z == last)
+    middle = jnp.logical_not(edge)
+    tokens = act.shape[0]
+    width = BLK
+    inv_block = 1.0 / math.sqrt(width)
+    inv_shard = 1.0 / math.sqrt(shards)
+    pieces = 2 * own
+
+    barrier = pltpu.get_barrier_semaphore()
+
+    def peer(m):
+        flipped = 1 - lax.rem(chip, 2) if m & 1 else lax.rem(chip, 2)
+        high = 1 - chip // 2 if m & 2 else chip // 2
+        return (high * 2 + flipped) * 2 + core
+
+    partner = chip * 2 + 1 - core
+    for m in (1, 2, 3):
+        pl.semaphore_signal(barrier, inc=1, device_id={"dp": peer(m)}, device_id_type=ALONG)
+    pl.semaphore_signal(barrier, inc=1, device_id={"dp": partner}, device_id_type=ALONG)
+
+    @pl.when(z > 0)
+    def _():
+        pl.semaphore_signal(barrier, inc=1, device_id={"shard": z - 1}, device_id_type=ALONG)
+
+    @pl.when(z < last)
+    def _():
+        pl.semaphore_signal(barrier, inc=1, device_id={"shard": z + 1}, device_id_type=ALONG)
+
+    row = lax.broadcasted_iota(jnp.int32, (width, width), 0)
+    col = lax.broadcasted_iota(jnp.int32, (width, width), 1)
+    both = row & col
+    count = both & 1
+    for level in range(1, width.bit_length() - 1):
+        count = count + ((both >> level) & 1)
+    table = (1 - 2 * (count & 1)).astype(jnp.float32).astype(jnp.bfloat16)
+
+    def contribution(owner, j):
+        lm = jnp.dot(picked[owner * own + j], table, preferred_element_type=jnp.float32)
+        return (lm * inv_block).astype(jnp.bfloat16).astype(jnp.float32) * inv_shard
+
+    def owner_of(way, t):
+        return jnp.where(way == 0, 1 - t, 2 + t)
+
+    def target(way):
+        return jnp.where(way == 0, z - 1, z + 1)
+
+    def s_copy(way, k):
+        return pltpu.make_async_remote_copy(
+            tx.at[way, k], rx.at[way, k], z_send.at[way, 3 + k], z_recv.at[way, 3 + k],
+            device_id={"shard": target(way)}, device_id_type=ALONG)
+
+    def g_copy(way, i):
+        return pltpu.make_async_remote_copy(
+            gtx.at[way, i], grx.at[way, i], z_send.at[way, i], z_recv.at[way, i],
+            device_id={"shard": target(way)}, device_id_type=ALONG)
+
+    def gpart(i):
+        r0, c0 = GP[i]
+        return part[r0 : r0 + 256, c0 : c0 + 256]
+
+    def ids_of(k):
+        return k // own, k % own
+
+    def units(c):
+        return pl.ds(FIRST[c], c + 1)
+
+    def a_copy(c, slot, who):
+        return pltpu.make_async_remote_copy(
+            gathered.at[d, units(c)], gathered.at[d, units(c)], a_send.at[c, slot], a_recv.at[c, slot],
+            device_id={"dp": who}, device_id_type=ALONG)
+
+    def a_recv_from(c, slot, who):
+        return pltpu.make_async_remote_copy(
+            gathered.at[who, units(c)], gathered.at[who, units(c)], a_send.at[c, slot], a_recv.at[c, slot],
+            device_id={"dp": who}, device_id_type=ALONG)
+
+    def w_copy(c, m):
+        return pltpu.make_async_remote_copy(
+            gathered.at[peer(m), units(c)], gathered.at[peer(m), units(c)],
+            w_send.at[c, m - 1], w_recv.at[c, m - 1],
+            device_id={"dp": partner}, device_id_type=ALONG)
+
+    def w_recv_from(c, m):
+        other = peer(m) + 1 - 2 * core
+        return pltpu.make_async_remote_copy(
+            gathered.at[other, units(c)], gathered.at[other, units(c)],
+            w_send.at[c, m - 1], w_recv.at[c, m - 1],
+            device_id={"dp": partner}, device_id_type=ALONG)
+
+    def spread(c):
+        for m in (1, 2, 3):
+            a_copy(c, m - 1, peer(m)).start()
+        a_copy(c, 3, partner).start()
+
+    def relay(c):
+        for m in (1, 2, 3):
+            a_recv_from(c, m - 1, peer(m)).wait_recv()
+            w_copy(c, m).start()
+
+    def settle(c):
+        a_recv_from(c, 3, partner).wait_recv()
+        for m in (1, 2, 3):
+            w_recv_from(c, m).wait_recv()
+        for m in (1, 2, 3):
+            a_copy(c, m - 1, peer(m)).wait_send()
+            w_copy(c, m).wait_send()
+        a_copy(c, 3, partner).wait_send()
+
+    def f_copy(c):
+        inward = jnp.where(z == 0, 1, last - 1)
+        return pltpu.make_async_remote_copy(
+            rrx.at[3, units(c)], gathered.at[d, units(c)], f_send.at[c], f_recv.at[c],
+            device_id={"shard": inward}, device_id_type=ALONG)
+
+    def f_recv_at():
+        def make(c):
+            outward = jnp.where(z == 1, 0, last)
+            return pltpu.make_async_remote_copy(
+                rrx.at[3, units(c)], gathered.at[d, units(c)], f_send.at[c], f_recv.at[c],
+                device_id={"shard": outward}, device_id_type=ALONG)
+        return make
+
+    part[...] = lax.dot_general(act[...], act[...], (((1,), (1,)), ((), ())), preferred_element_type=jnp.float32)
+
+    @pl.when(edge)
+    def _():
+        pl.semaphore_wait(barrier, 5)
+
+    @pl.when(middle)
+    def _():
+        pl.semaphore_wait(barrier, 6)
+
+    @pl.when(edge)
+    def _():
+        out_way = jnp.where(z == 0, 1, 0)
+        in_way = 1 - out_way
+        for i in range(3):
+            gtx[out_way, i] = gpart(i).astype(jnp.bfloat16)
+            g_copy(out_way, i).start()
+
+        def push(k, carry):
+            t, j = k // own, lax.rem(k, own)
+            tx[out_way, k] = contribution(owner_of(out_way, t), j).astype(jnp.bfloat16)
+            s_copy(out_way, k).start()
+            return carry
+
+        lax.fori_loop(0, pieces, push, 0)
+
+        for i in range(3):
+            r0, c0 = GP[i]
+            pltpu.make_async_remote_copy(
+                gtx.at[in_way, i], grx.at[in_way, i], z_send.at[in_way, i], z_recv.at[in_way, i],
+                device_id={"shard": target(out_way)}, device_id_type=ALONG).wait_recv()
+            block = (grx[in_way, i].astype(jnp.float32) + gpart(i)).astype(jnp.bfloat16)
+            full[r0 : r0 + 256, c0 : c0 + 256] = block
+            if r0 != c0:
+                full[c0 : c0 + 256, r0 : r0 + 256] = block.T
+
+        def where(q):
+            t, c = q // CHUNKS, q % CHUNKS
+            return t, c, pl.ds(10 * t + FIRST[c], c + 1)
+
+        def p_copy(q):
+            t, c, us = where(q)
+            return pltpu.make_async_remote_copy(
+                halves.at[1 - core, us], prx.at[us], p_send.at[q], p_recv.at[q],
+                device_id={"dp": partner}, device_id_type=ALONG)
+
+        def r_copy(q, m):
+            t, c, us = where(q)
+            return pltpu.make_async_remote_copy(
+                rtx.at[peer(m) // 2, us], rrx.at[m - 1, us], r_send.at[q, m - 1], r_recv.at[q, m - 1],
+                device_id={"dp": peer(m)}, device_id_type=ALONG)
+
+        def step_a(q):
+            t, c, us = where(q)
+            for side in range(2):
+                j = 2 * c + side
+                k = own * t + j
+                mine = contribution(owner_of(in_way, t), j)
+                pltpu.make_async_remote_copy(
+                    tx.at[in_way, k], rx.at[in_way, k], z_send.at[in_way, 3 + k], z_recv.at[in_way, 3 + k],
+                    device_id={"shard": target(out_way)}, device_id_type=ALONG).wait_recv()
+                done = (rx[in_way, k].astype(jnp.float32) + mine).astype(jnp.bfloat16)
+                sketch[t, :, width * j : width * (j + 1)] = done
+            cols = sketch[t, :, 256 * c : 256 * (c + 1)]
+            weighted = jnp.dot(full[...], cols, preferred_element_type=jnp.float32).astype(jnp.bfloat16)
+            for i in range(c + 1):
+                unit = lax.dot_general(
+                    sketch[t, :, 256 * i : 256 * (i + 1)], weighted, (((0,), (0,)), ((), ())),
+                    preferred_element_type=jnp.float32)
+                halves[0, 10 * t + FIRST[c] + i] = unit[:128]
+                halves[1, 10 * t + FIRST[c] + i] = unit[128:]
+            p_copy(q).start()
+
+        def step_b(q):
+            t, c, us = where(q)
+            p_copy(q).wait_recv()
+            for i in range(c + 1):
+                u = 10 * t + FIRST[c] + i
+                total = (halves[core, u] + prx[u]).astype(jnp.bfloat16)
+                for n in range(4):
+                    rtx[n, u] = total[32 * n : 32 * (n + 1)]
+            for m in (1, 2, 3):
+                r_copy(q, m).start()
+
+        def step_c(q):
+            t, c, us = where(q)
+            for m in (1, 2, 3):
+                r_copy(q, m).wait_recv()
+            for i in range(c + 1):
+                u = 10 * t + FIRST[c] + i
+                total = rtx[chip, u].astype(jnp.float32)
+                for m in range(3):
+                    total = total + rrx[m, u].astype(jnp.float32)
+                total = (total * (1.0 / (parts * tokens * act.shape[1] * shards))).astype(jnp.bfloat16)
+                if t == 0:
+                    rrx[3, FIRST[c] + i] = total
+                else:
+                    gathered[d, FIRST[c] + i] = total
+            if t == 0:
+                f_copy(c).start()
+            else:
+                spread(c)
+
+        def step_d(q):
+            if q >= CHUNKS:
+                relay(q - CHUNKS)
+
+        steps = 2 * CHUNKS
+        for q in range(steps + 3):
+            if 0 <= q - 1 < steps:
+                step_b(q - 1)
+            if 0 <= q - 2 < steps:
+                step_c(q - 2)
+            if 0 <= q - 3 < steps:
+                step_d(q - 3)
+            if q < steps:
+                step_a(q)
+        for c in range(CHUNKS):
+            settle(c)
+            f_copy(c).wait_send()
+        for q in range(steps):
+            p_copy(q).wait_send()
+            for m in (1, 2, 3):
+                r_copy(q, m).wait_send()
+        for i in range(3):
+            g_copy(out_way, i).wait_send()
+
+        def drain(k, carry):
+            s_copy(out_way, k).wait_send()
+            return carry
+
+        lax.fori_loop(0, pieces, drain, 0)
+
+    @pl.when(middle)
+    def _():
+        near = jnp.where(z == 1, 1, 0)
+        far = 1 - near
+
+        def pass_g(way, i):
+            g_copy(way, i).wait_recv()
+            gtx[way, i] = (grx[way, i].astype(jnp.float32) + gpart(i)).astype(jnp.bfloat16)
+            g_copy(way, i).start()
+
+        def pass_s(way, k):
+            t, j = k // own, lax.rem(k, own)
+            mine = contribution(owner_of(way, t), j)
+            s_copy(way, k).wait_recv()
+            tx[way, k] = (rx[way, k].astype(jnp.float32) + mine).astype(jnp.bfloat16)
+            s_copy(way, k).start()
+
+        pass_g(near, 0)
+        pass_g(near, 1)
+        pass_g(far, 0)
+        pass_g(near, 2)
+        pass_g(far, 1)
+        pass_s(near, 0)
+        pass_g(far, 2)
+
+        def both_ways(k, carry):
+            pass_s(near, k)
+            pass_s(far, k - 1)
+            return carry
+
+        lax.fori_loop(1, pieces, both_ways, 0)
+        pass_s(far, pieces - 1)
+        arrival = f_recv_at()
+        for c in range(CHUNKS):
+            arrival(c).wait_recv()
+            spread(c)
+        for c in range(CHUNKS):
+            relay(c)
+        for c in range(CHUNKS):
+            settle(c)
+        for way in range(2):
+            for i in range(3):
+                g_copy(way, i).wait_send()
+
+        def drain(k, carry):
+            s_copy(0, k).wait_send()
+            s_copy(1, k).wait_send()
+            return carry
+
+        lax.fori_loop(0, pieces, drain, 0)
+
+    out[...] = gathered[...]
+
+
+def assemble_kernel(got, out):
+    for c in range(CHUNKS):
+        for i in range(c + 1):
+            u = FIRST[c] + i
+            rows = [got[2 * n + h, u] for h in range(2) for n in range(4)]
+            unit = jnp.concatenate(rows, axis=0).astype(jnp.float32)
+            out[256 * i : 256 * (i + 1), 256 * c : 256 * (c + 1)] = unit
+            if i != c:
+                out[256 * c : 256 * (c + 1), 256 * i : 256 * (i + 1)] = unit.T
+
+
+def fast_body(shards, parts, activations, out_grads, sign_bits, block_ids):
+    tokens, columns = out_grads.shape
+    per = columns // BLK
+    own = block_ids.shape[1]
+    vmem = pl.BlockSpec(memory_space=pltpu.VMEM)
+    bf, f32 = jnp.bfloat16, jnp.float32
+    dma = pltpu.SemaphoreType.DMA
+    number = shards * own
+    picked = pl.pallas_call(
+        functools.partial(pick_kernel, shards, own, per),
+        out_shape=jax.ShapeDtypeStruct((number, tokens, BLK), bf),
+        in_specs=[pl.BlockSpec(memory_space=pltpu.SMEM), vmem, pl.BlockSpec(memory_space=pl.ANY)],
+        out_specs=pl.BlockSpec(memory_space=pl.ANY),
+        scratch_shapes=[pltpu.VMEM((number, tokens, BLK), bf), dma((number,)), dma((number,))],
+        name="pick",
+    )(block_ids.reshape(-1), sign_bits.reshape(1, columns), out_grads)
+    got = pl.pallas_call(
+        functools.partial(mix_kernel, shards, parts, own),
+        out_shape=jax.ShapeDtypeStruct((parts, 10, 32, 256), bf),
+        in_specs=[vmem, vmem],
+        out_specs=vmem,
+        scratch_shapes=[
+            pltpu.VMEM((2, 2 * own, tokens, BLK), bf),
+            pltpu.VMEM((2, 2 * own, tokens, BLK), bf),
+            pltpu.VMEM((2, 3, 256, 256), bf),
+            pltpu.VMEM((2, 3, 256, 256), bf),
+            pltpu.VMEM((tokens, tokens), f32),
+            pltpu.VMEM((tokens, tokens), bf),
+            pltpu.VMEM((2, tokens, own * BLK), bf),
+            pltpu.VMEM((2, 20, 128, 256), f32),
+            pltpu.VMEM((20, 128, 256), f32),
+            pltpu.VMEM((4, 20, 32, 256), bf),
+            pltpu.VMEM((4, 20, 32, 256), bf),
+            pltpu.VMEM((parts, 10, 32, 256), bf),
+            dma((2, 3 + 2 * own)), dma((2, 3 + 2 * own)),
+            dma((8,)), dma((8,)),
+            dma((8, 3)), dma((8, 3)),
+            dma((4,)), dma((4,)),
+            dma((4, 4)), dma((4, 4)),
+            dma((4, 3)), dma((4, 3)),
+        ],
+        compiler_params=pltpu.CompilerParams(collective_id=0, has_side_effects=True, vmem_limit_bytes=56 * 2**20),
+        name="mix",
+    )(activations, picked)
+    return pl.pallas_call(
+        assemble_kernel,
+        out_shape=jax.ShapeDtypeStruct((own * BLK, own * BLK), f32),
+        in_specs=[vmem],
+        out_specs=vmem,
+        name="assemble",
+    )(got)
+
+
 def solution(mesh):
     in_specs = (P("dp", "shard"), P("dp", "shard"), P("shard"), P())
     out_specs = P("shard", None)
-    return jax.shard_map(body, mesh=mesh, in_specs=in_specs, out_specs=out_specs, check_vma=False)
+    shards, parts = mesh.shape["shard"], mesh.shape["dp"]
+    chosen = functools.partial(fast_body, shards, parts) if (shards, parts) == (4, 8) else body
+    return jax.shard_map(chosen, mesh=mesh, in_specs=in_specs, out_specs=out_specs, check_vma=False)

time: 691 us -> 101 us (0.15)
  waiting for transfers between devices: 553 us -> 0 us
  Pallas kernels: 0 us -> 97.7 us
  blocking collectives: 63.9 us -> 0 us
  other arithmetic: 29.5 us -> 0 us
  between operations: 13.5 us -> 0.02 us
  starting transfers between devices: 10.5 us -> 0 us
  matrix products: 10.1 us -> 0 us
  local copies, waits for them, and re-layouts: 10 us -> 2.59 us
    ppermute x2 -> x0, waiting for transfers between devices: 472 us -> none  [partner_2(): lax.ppermute(x, axis, [(i, i ^ 1 << distance) for i in range(lax.axis_siz...]
    pallas_call x0 -> x3, Pallas kernels: none -> 97.7 us  [the longest x1 88.5 us: fast_body(): pl.pallas_call(functools.partial(mix_kernel, shards, parts, own), out_sha...]
    psum x1 -> x0, waiting for transfers between devices: 81.2 us -> none  [body(): summed = lax.psum(block_gram, 'dp')]
    psum x1 -> x0, blocking collectives: 63.9 us -> none  [body(): token_gram = lax.psum(partial_gram, 'shard').astype(jnp.bfloat16)]
    select_n x5 -> x0, other arithmetic: 10.8 us -> none  [the longest x1 10.6 us: body(): running = jnp.where(upper, partner - running, running + partner)]
    dot_general x4 -> x0, matrix products: 10.1 us -> none  [the longest x1 4.27 us: body(): jnp.einsum('tbj,jk->btk', flipped, block_table, preferred_element_type=jn...]
    convert_element_type x3 -> x0, other arithmetic: 9.07 us -> none  [the longest x1 9.05 us: body(): mixed = (running * inv_shard).astype(jnp.bfloat16)]
  transfers between devices with their start and end apart: 4 -> 0, of which waited for: 3 -> 0; matrix products, arithmetic and copies ran while one was open for 0% -> 0% of each run, Pallas kernels for 0% -> 0%
where the time goes in v1:
time: 101 us; the launch traced here: 100 us
  Pallas kernels  97.7 us (97%)
  local copies, waits for them, and re-layouts  2.59 us (3%)
    pallas_call x1, Pallas kernels, fast_body(): pl.pallas_call(functools.partial(mix_kernel, shards, parts, own), out_sha...  88.5 us
    pallas_call x1, Pallas kernels, fast_body(): pl.pallas_call(functools.partial(pick_kernel, shards, own, per), out_shap...  5.56 us
    pallas_call x1, Pallas kernels, fast_body(): pl.pallas_call(assemble_kernel, out_shape=jax.ShapeDtypeStruct((own * BLK...  3.66 us

profile of v1, /device:TPU:0, one launch (start us, length us, event | category | flops | bytes accessed | tf_op | source)
XLA Modules:
  0.0 100.3 jit_solution(17555009375397872775)
XLA Ops:
  0.0 1.3 %reshape.6.ids = s32[32]{0:T(128)} reshape(s32[4,8]{1,0:T(4,128)} %param.7) | data formatting | bytes 256 | tf_op jit(solution)/shard_map/reshape | solution.py:471
  1.3 1.3 %reshape.7.bits = s32[1,3584]{1,0:T(1,128)} reshape(s32[3584]{0:T(1024)} %param.6) | data formatting | bytes 28672 | tf_op jit(solution)/shard_map/reshape | solution.py:471
  2.6 5.6 %pick.1.picked = bf16[32,512,128]{2,1,0:T(8,128)(2,1)} custom-call(s32[32]{0:T(128)} %reshape.6.ids, s32[1,3584]{1,0:T(1,128)} %reshape.7.bits, bf16[512,3584]{1,0:T(8,128)(2,1)} %grads.1), custom_call_target="tpu_custom_call" | custom-call | tf_op jit(solution)/shard_map/pick/pallas_call | solution.py:464
  8.2 88.5 %mix.1.got = bf16[8,10,32,256]{3,2,1,0:T(8,128)(2,1)} custom-call(bf16[512,1024]{1,0:T(8,128)(2,1)} %act.1, bf16[32,512,128]{2,1,0:T(8,128)(2,1)} %pick.1.picked), custom_call_target="tpu_custom_call" | custom-call | tf_op jit(solution)/shard_map/mix/pallas_call | solution.py:472
  96.6 3.7 %assemble.1 = f32[1024,1024]{1,0:T(8,128)} custom-call(bf16[8,10,32,256]{3,2,1,0:T(8,128)(2,1)} %mix.1.got), custom_call_target="tpu_custom_call" | custom-call | tf_op jit(solution)/shard_map/assemble/pallas_call | solution.py:500

commit v2 on v1

--- a/solution.py
+++ b/solution.py
@@ -76,51 +76,36 @@
 
 
 ALONG = pl.DeviceIdType.MESH
-CHUNKS = 4
-GP = ((0, 0), (256, 256), (256, 0))
-FIRST = (0, 1, 3, 6, 10)
-
-
-def pick_kernel(shards, own, per, ids, bits, grads, out, held, i_sem, o_sem):
+SPANS = ((0, 2), (2, 4), (4, 6), (6, 7), (7, 8))
+CHUNKS = len(SPANS)
+FIRST = tuple(sum((hi - lo) * hi for lo, hi in SPANS[:c]) for c in range(CHUNKS + 1))
+UNITS = FIRST[CHUNKS]
+TRIANGLE = tuple((i, j) for i in range(4) for j in range(i + 1))
+GSPANS = ((0, 4), (4, 7), (7, 10))
+
+
+def pick_kernel(shards, own, per, ids, bits, grads, out):
     z = lax.axis_index("shard")
     width = BLK
     number = shards * own
 
     def start_of(p):
-        block = ids[p]
+        block = ids[p // own, lax.rem(p, own)]
         r = block // per
         return r, pl.multiple_of((block - r * per) * width, width)
 
-    def fetch(p):
-        return pltpu.make_async_copy(grads.at[:, pl.ds(start_of(p)[1], width)], held.at[p], i_sem.at[p])
-
-    def put(p):
-        return pltpu.make_async_copy(held.at[p], out.at[p], o_sem.at[p])
-
-    def first(p, carry):
-        fetch(p).start()
-        return carry
-
-    def middle(p, carry):
+    def take(p, carry):
         r, start = start_of(p)
         common = r & z
         odd = common & 1
         for level in range(1, shards.bit_length() - 1):
             odd = odd + ((common >> level) & 1)
         sign = 1 - 2 * (odd & 1)
-        signs = ((1 - 2 * bits[:, pl.ds(start, width)]) * sign).astype(jnp.float32).astype(jnp.bfloat16)
-        fetch(p).wait()
-        held[p] = held[p] * signs
-        put(p).start()
+        signs = ((1 - 2 * bits[pl.ds(start, width)].reshape(1, width)) * sign).astype(jnp.float32).astype(jnp.bfloat16)
+        out[p] = grads[:, pl.ds(start, width)] * signs
         return carry
 
-    def end(p, carry):
-        put(p).wait()
-        return carry
-
-    lax.fori_loop(0, number, first, 0)
-    lax.fori_loop(0, number, middle, 0)
-    lax.fori_loop(0, number, end, 0)
+    lax.fori_loop(0, number, take, 0)
 
 
 def mix_kernel(
@@ -185,19 +170,17 @@
             device_id={"shard": target(way)}, device_id_type=ALONG)
 
     def g_copy(way, i):
-        return pltpu.make_async_remote_copy(
-            gtx.at[way, i], grx.at[way, i], z_send.at[way, i], z_recv.at[way, i],
+        lo, hi = GSPANS[i]
+        return pltpu.make_async_remote_copy(
+            gtx.at[way, lo:hi], grx.at[way, lo:hi], z_send.at[way, i], z_recv.at[way, i],
             device_id={"shard": target(way)}, device_id_type=ALONG)
 
-    def gpart(i):
-        r0, c0 = GP[i]
-        return part[r0 : r0 + 256, c0 : c0 + 256]
-
-    def ids_of(k):
-        return k // own, k % own
+    def gpart(n):
+        i, j = TRIANGLE[n]
+        return part[128 * i : 128 * (i + 1), 128 * j : 128 * (j + 1)]
 
     def units(c):
-        return pl.ds(FIRST[c], c + 1)
+        return pl.ds(FIRST[c], FIRST[c + 1] - FIRST[c])
 
     def a_copy(c, slot, who):
         return pltpu.make_async_remote_copy(
@@ -270,7 +253,8 @@
         out_way = jnp.where(z == 0, 1, 0)
         in_way = 1 - out_way
         for i in range(3):
-            gtx[out_way, i] = gpart(i).astype(jnp.bfloat16)
+            for n in range(*GSPANS[i]):
+                gtx[out_way, n] = gpart(n).astype(jnp.bfloat16)
             g_copy(out_way, i).start()
 
         def push(k, carry):
@@ -282,18 +266,20 @@
         lax.fori_loop(0, pieces, push, 0)
 
         for i in range(3):
-            r0, c0 = GP[i]
+            lo, hi = GSPANS[i]
             pltpu.make_async_remote_copy(
-                gtx.at[in_way, i], grx.at[in_way, i], z_send.at[in_way, i], z_recv.at[in_way, i],
+                gtx.at[in_way, lo:hi], grx.at[in_way, lo:hi], z_send.at[in_way, i], z_recv.at[in_way, i],
                 device_id={"shard": target(out_way)}, device_id_type=ALONG).wait_recv()
-            block = (grx[in_way, i].astype(jnp.float32) + gpart(i)).astype(jnp.bfloat16)
-            full[r0 : r0 + 256, c0 : c0 + 256] = block
-            if r0 != c0:
-                full[c0 : c0 + 256, r0 : r0 + 256] = block.T
+            for n in range(lo, hi):
+                r, c = TRIANGLE[n]
+                block = (grx[in_way, n].astype(jnp.float32) + gpart(n)).astype(jnp.bfloat16)
+                full[128 * r : 128 * (r + 1), 128 * c : 128 * (c + 1)] = block
+                if r != c:
+                    full[128 * c : 128 * (c + 1), 128 * r : 128 * (r + 1)] = block.T
 
         def where(q):
             t, c = q // CHUNKS, q % CHUNKS
-            return t, c, pl.ds(10 * t + FIRST[c], c + 1)
+            return t, c, pl.ds(UNITS * t + FIRST[c], FIRST[c + 1] - FIRST[c])
 
         def p_copy(q):
             t, c, us = where(q)
@@ -309,8 +295,8 @@
 
         def step_a(q):
             t, c, us = where(q)
-            for side in range(2):
-                j = 2 * c + side
+            lo, hi = SPANS[c]
+            for j in range(lo, hi):
                 k = own * t + j
                 mine = contribution(owner_of(in_way, t), j)
                 pltpu.make_async_remote_copy(
@@ -318,24 +304,27 @@
                     device_id={"shard": target(out_way)}, device_id_type=ALONG).wait_recv()
                 done = (rx[in_way, k].astype(jnp.float32) + mine).astype(jnp.bfloat16)
                 sketch[t, :, width * j : width * (j + 1)] = done
-            cols = sketch[t, :, 256 * c : 256 * (c + 1)]
+            cols = sketch[t, :, width * lo : width * hi]
             weighted = jnp.dot(full[...], cols, preferred_element_type=jnp.float32).astype(jnp.bfloat16)
-            for i in range(c + 1):
+            for top in range(0, hi, 2):
+                end = min(top + 2, hi)
                 unit = lax.dot_general(
-                    sketch[t, :, 256 * i : 256 * (i + 1)], weighted, (((0,), (0,)), ((), ())),
+                    sketch[t, :, width * top : width * end], weighted, (((0,), (0,)), ((), ())),
                     preferred_element_type=jnp.float32)
-                halves[0, 10 * t + FIRST[c] + i] = unit[:128]
-                halves[1, 10 * t + FIRST[c] + i] = unit[128:]
+                for i in range(top, end):
+                    for j in range(lo, hi):
+                        u = UNITS * t + FIRST[c] + (j - lo) * hi + i
+                        block = unit[128 * (i - top) : 128 * (i - top + 1), width * (j - lo) : width * (j - lo + 1)]
+                        halves[0, u] = block[:64]
+                        halves[1, u] = block[64:]
             p_copy(q).start()
 
         def step_b(q):
             t, c, us = where(q)
             p_copy(q).wait_recv()
-            for i in range(c + 1):
-                u = 10 * t + FIRST[c] + i
-                total = (halves[core, u] + prx[u]).astype(jnp.bfloat16)
-                for n in range(4):
-                    rtx[n, u] = total[32 * n : 32 * (n + 1)]
+            total = (halves[core, us] + prx[us]).astype(jnp.bfloat16)
+            for n in range(4):
+                rtx[n, us] = total[:, 16 * n : 16 * (n + 1)]
             for m in (1, 2, 3):
                 r_copy(q, m).start()
 
@@ -343,16 +332,14 @@
             t, c, us = where(q)
             for m in (1, 2, 3):
                 r_copy(q, m).wait_recv()
-            for i in range(c + 1):
-                u = 10 * t + FIRST[c] + i
-                total = rtx[chip, u].astype(jnp.float32)
-                for m in range(3):
-                    total = total + rrx[m, u].astype(jnp.float32)
-                total = (total * (1.0 / (parts * tokens * act.shape[1] * shards))).astype(jnp.bfloat16)
-                if t == 0:
-                    rrx[3, FIRST[c] + i] = total
-                else:
-                    gathered[d, FIRST[c] + i] = total
+            total = rtx[chip, us].astype(jnp.float32)
+            for m in range(3):
+                total = total + rrx[m, us].astype(jnp.float32)
+            total = (total * (1.0 / (parts * tokens * act.shape[1] * shards))).astype(jnp.bfloat16)
+            if t == 0:
+                rrx[3, units(c)] = total
+            else:
+                gathered[d, units(c)] = total
             if t == 0:
                 f_copy(c).start()
             else:
@@ -395,7 +382,8 @@
 
         def pass_g(way, i):
             g_copy(way, i).wait_recv()
-            gtx[way, i] = (grx[way, i].astype(jnp.float32) + gpart(i)).astype(jnp.bfloat16)
+            for n in range(*GSPANS[i]):
+                gtx[way, n] = (grx[way, n].astype(jnp.float32) + gpart(n)).astype(jnp.bfloat16)
             g_copy(way, i).start()
 
         def pass_s(way, k):
@@ -443,14 +431,15 @@
 
 
 def assemble_kernel(got, out):
-    for c in range(CHUNKS):
-        for i in range(c + 1):
-            u = FIRST[c] + i
-            rows = [got[2 * n + h, u] for h in range(2) for n in range(4)]
-            unit = jnp.concatenate(rows, axis=0).astype(jnp.float32)
-            out[256 * i : 256 * (i + 1), 256 * c : 256 * (c + 1)] = unit
-            if i != c:
-                out[256 * c : 256 * (c + 1), 256 * i : 256 * (i + 1)] = unit.T
+    for c, (lo, hi) in enumerate(SPANS):
+        for j in range(lo, hi):
+            for i in range(hi):
+                u = FIRST[c] + (j - lo) * hi + i
+                rows = [got[2 * n + h, u] for h in range(2) for n in range(4)]
+                unit = jnp.concatenate(rows, axis=0).astype(jnp.float32)
+                out[128 * i : 128 * (i + 1), 128 * j : 128 * (j + 1)] = unit
+                if i < lo:
+                    out[128 * j : 128 * (j + 1), 128 * i : 128 * (i + 1)] = unit.T
 
 
 def fast_body(shards, parts, activations, out_grads, sign_bits, block_ids):
@@ -464,37 +453,37 @@
     picked = pl.pallas_call(
         functools.partial(pick_kernel, shards, own, per),
         out_shape=jax.ShapeDtypeStruct((number, tokens, BLK), bf),
-        in_specs=[pl.BlockSpec(memory_space=pltpu.SMEM), vmem, pl.BlockSpec(memory_space=pl.ANY)],
-        out_specs=pl.BlockSpec(memory_space=pl.ANY),
-        scratch_shapes=[pltpu.VMEM((number, tokens, BLK), bf), dma((number,)), dma((number,))],
+        in_specs=[pl.BlockSpec(memory_space=pltpu.SMEM), vmem, vmem],
+        out_specs=vmem,
+        compiler_params=pltpu.CompilerParams(vmem_limit_bytes=12 * 2**20),
         name="pick",
-    )(block_ids.reshape(-1), sign_bits.reshape(1, columns), out_grads)
+    )(block_ids, sign_bits, out_grads)
     got = pl.pallas_call(
         functools.partial(mix_kernel, shards, parts, own),
-        out_shape=jax.ShapeDtypeStruct((parts, 10, 32, 256), bf),
+        out_shape=jax.ShapeDtypeStruct((parts, UNITS, 16, BLK), bf),
         in_specs=[vmem, vmem],
         out_specs=vmem,
         scratch_shapes=[
             pltpu.VMEM((2, 2 * own, tokens, BLK), bf),
             pltpu.VMEM((2, 2 * own, tokens, BLK), bf),
-            pltpu.VMEM((2, 3, 256, 256), bf),
-            pltpu.VMEM((2, 3, 256, 256), bf),
+            pltpu.VMEM((2, 10, 128, 128), bf),
+            pltpu.VMEM((2, 10, 128, 128), bf),
             pltpu.VMEM((tokens, tokens), f32),
             pltpu.VMEM((tokens, tokens), bf),
             pltpu.VMEM((2, tokens, own * BLK), bf),
-            pltpu.VMEM((2, 20, 128, 256), f32),
-            pltpu.VMEM((20, 128, 256), f32),
-            pltpu.VMEM((4, 20, 32, 256), bf),
-            pltpu.VMEM((4, 20, 32, 256), bf),
-            pltpu.VMEM((parts, 10, 32, 256), bf),
+            pltpu.VMEM((2, 2 * UNITS, 64, BLK), f32),
+            pltpu.VMEM((2 * UNITS, 64, BLK), f32),
+            pltpu.VMEM((4, 2 * UNITS, 16, BLK), bf),
+            pltpu.VMEM((4, 2 * UNITS, 16, BLK), bf),
+            pltpu.VMEM((parts, UNITS, 16, BLK), bf),
             dma((2, 3 + 2 * own)), dma((2, 3 + 2 * own)),
-            dma((8,)), dma((8,)),
-            dma((8, 3)), dma((8, 3)),
-            dma((4,)), dma((4,)),
-            dma((4, 4)), dma((4, 4)),
-            dma((4, 3)), dma((4, 3)),
+            dma((2 * CHUNKS,)), dma((2 * CHUNKS,)),
+            dma((2 * CHUNKS, 3)), dma((2 * CHUNKS, 3)),
+            dma((CHUNKS,)), dma((CHUNKS,)),
+            dma((CHUNKS, 4)), dma((CHUNKS, 4)),
+            dma((CHUNKS, 3)), dma((CHUNKS, 3)),
         ],
-        compiler_params=pltpu.CompilerParams(collective_id=0, has_side_effects=True, vmem_limit_bytes=56 * 2**20),
+        compiler_params=pltpu.CompilerParams(collective_id=0, has_side_effects=True, vmem_limit_bytes=40 * 2**20),
         name="mix",
     )(activations, picked)
     return pl.pallas_call(
@@ -502,6 +491,7 @@
         out_shape=jax.ShapeDtypeStruct((own * BLK, own * BLK), f32),
         in_specs=[vmem],
         out_specs=vmem,
+        compiler_params=pltpu.CompilerParams(vmem_limit_bytes=16 * 2**20),
         name="assemble",
     )(got)
 

time: 101 us -> 92.9 us (0.920)
  Pallas kernels: 97.7 us -> 89.2 us
    pallas_call x1, Pallas kernels: 88.5 us -> 84.6 us  [fast_body(): pl.pallas_call(functools.partial(mix_kernel, shards, parts, own), out_sha...]
    pallas_call x1, Pallas kernels: 5.56 us -> 2.1 us  [fast_body(): pl.pallas_call(functools.partial(pick_kernel, shards, own, per), out_shap...]
    unnamed x0 -> x8, local copies, waits for them, and re-layouts: none -> 3.44 us
    reshape x2 -> x0, local copies, waits for them, and re-layouts: 2.59 us -> none  [the longest x1 1.32 us: fast_body(): sign_bits.reshape(1, columns)]
    pallas_call x1, Pallas kernels: 3.66 us -> 2.43 us  [fast_body(): pl.pallas_call(assemble_kernel, out_shape=jax.ShapeDtypeStruct((own * BLK...]
where the time goes in v2:
time: 92.9 us; the launch traced here: 92.6 us
  Pallas kernels  89.2 us (96%)
  local copies, waits for them, and re-layouts  3.44 us (4%)
    pallas_call x1, Pallas kernels, fast_body(): pl.pallas_call(functools.partial(mix_kernel, shards, parts, own), out_sha...  84.6 us
    unnamed x8, local copies, waits for them, and re-layouts  3.44 us
    pallas_call x1, Pallas kernels, fast_body(): pl.pallas_call(assemble_kernel, out_shape=jax.ShapeDtypeStruct((own * BLK...  2.43 us
    pallas_call x1, Pallas kernels, fast_body(): pl.pallas_call(functools.partial(pick_kernel, shards, own, per), out_shap...  2.1 us

profile of v2, /device:TPU:0, one launch (start us, length us, event | category | flops | bytes accessed | tf_op | source)
XLA Modules:
  0.0 92.6 jit_solution(2183281635607318588)
XLA Ops:
  0.0 0.0 copy-start
  0.0 2.0 %copy-done = bf16[512,3584]{1,0:T(8,128)(2,1)S(1)} copy-done((bf16[512,3584]{1,0:T(8,128)(2,1)S(1)}, bf16[512,3584]{1,0:T(8,128)(2,1)}, u32[]{:S(2)}) %copy-start) | copy-done | bytes 3670040
  2.0 0.0 copy-start.2
  2.0 0.7 copy-done.2
  2.8 0.0 copy-start.3
  2.8 0.7 copy-done.3
  3.4 0.0 copy-start.1
  3.4 2.1 %pick.1.picked = bf16[32,512,128]{2,1,0:T(8,128)(2,1)S(1)} custom-call(s32[4,8]{1,0:T(4,128)S(1)} %copy-done.3, s32[3584]{0:T(1024)S(1)} %copy-done.2, bf16[512,3584]{1,0:T(8,128)(2,1)S(1)} %copy-done), custom_call_target="tpu_custom_call" | custom-call | tf_op jit(solution)/shard_map/pick/pallas_call | solution.py:453
  5.6 0.0 copy-done.1
  5.6 84.6 %mix.1.got = bf16[8,39,16,128]{3,2,1,0:T(8,128)(2,1)S(1)} custom-call(bf16[512,1024]{1,0:T(8,128)(2,1)S(1)} %copy-done.1, bf16[32,512,128]{2,1,0:T(8,128)(2,1)S(1)} %pick.1.picked), custom_call_target="tpu_custom_call" | custom-call | tf_op jit(solution)/shard_map/mix/pallas_call | solution.py:461
  90.2 2.4 %assemble.1 = f32[1024,1024]{1,0:T(8,128)} custom-call(bf16[8,39,16,128]{3,2,1,0:T(8,128)(2,1)S(1)} %mix.1.got), custom_call_target="tpu_custom_call" | custom-call | tf_op jit(solution)/shard_map/assemble/pallas_call | solution.py:489
Async XLA Ops:
  0.0 2.0 %copy-start = (bf16[512,3584]{1,0:T(8,128)(2,1)S(1)}, bf16[512,3584]{1,0:T(8,128)(2,1)}, u32[]{:S(2)}) copy-start(bf16[512,3584]{1,0:T(8,128)(2,1)} %grads.1) | copy-start | bytes 11010052
  2.0 0.7 copy-start.2
  2.8 0.7 copy-start.3
  3.4 2.1 %copy-start.1 = (bf16[512,1024]{1,0:T(8,128)(2,1)S(1)}, bf16[512,1024]{1,0:T(8,128)(2,1)}, u32[]{:S(2)}) copy-start(bf16[512,1024]{1,0:T(8,128)(2,1)} %act.1) | copy-start | bytes 3145732

commit v3 on v2

--- a/solution.py
+++ b/solution.py
@@ -81,31 +81,45 @@
 FIRST = tuple(sum((hi - lo) * hi for lo, hi in SPANS[:c]) for c in range(CHUNKS + 1))
 UNITS = FIRST[CHUNKS]
 TRIANGLE = tuple((i, j) for i in range(4) for j in range(i + 1))
-GSPANS = ((0, 4), (4, 7), (7, 10))
-
-
-def pick_kernel(shards, own, per, ids, bits, grads, out):
+GSPANS = ((0, 2), (2, 4), (4, 6), (6, 8), (8, 10))
+GS = len(GSPANS)
+
+
+def pick_kernel(shards, own, per, ids_in, bits_in, grads, out, ids, bits, held, sems):
     z = lax.axis_index("shard")
     width = BLK
     number = shards * own
-
-    def start_of(p):
-        block = ids[p // own, lax.rem(p, own)]
-        r = block // per
-        return r, pl.multiple_of((block - r * per) * width, width)
-
-    def take(p, carry):
-        r, start = start_of(p)
-        common = r & z
-        odd = common & 1
-        for level in range(1, shards.bit_length() - 1):
-            odd = odd + ((common >> level) & 1)
-        sign = 1 - 2 * (odd & 1)
-        signs = ((1 - 2 * bits[pl.ds(start, width)].reshape(1, width)) * sign).astype(jnp.float32).astype(jnp.bfloat16)
-        out[p] = grads[:, pl.ds(start, width)] * signs
-        return carry
-
-    lax.fori_loop(0, number, take, 0)
+    cuts = held.shape[0]
+    rows = held.shape[1]
+
+    def fetch(n):
+        return pltpu.make_async_copy(grads.at[pl.ds(rows * n, rows)], held.at[n], sems.at[n])
+
+    early = (pltpu.make_async_copy(ids_in, ids, sems.at[cuts]), pltpu.make_async_copy(bits_in, bits, sems.at[cuts + 1]))
+    for copy in early:
+        copy.start()
+    for n in range(cuts):
+        fetch(n).start()
+    for copy in early:
+        copy.wait()
+    for n in range(cuts):
+        fetch(n).wait()
+
+        def take(p, carry):
+            block = ids[p // own, lax.rem(p, own)]
+            r = block // per
+            start = pl.multiple_of((block - r * per) * width, width)
+            common = r & z
+            odd = common & 1
+            for level in range(1, shards.bit_length() - 1):
+                odd = odd + ((common >> level) & 1)
+            sign = 1 - 2 * (odd & 1)
+            flips = (1 - 2 * bits[pl.ds(start, width)].reshape(1, width)) * sign
+            flips = flips.astype(jnp.float32).astype(jnp.bfloat16)
+            out[p, rows * n : rows * (n + 1)] = held[n, :, pl.ds(start, width)] * flips
+            return carry
+
+        lax.fori_loop(0, number, take, 0, unroll=4)
 
 
 def mix_kernel(
@@ -164,10 +178,16 @@
     def target(way):
         return jnp.where(way == 0, z - 1, z + 1)
 
-    def s_copy(way, k):
-        return pltpu.make_async_remote_copy(
-            tx.at[way, k], rx.at[way, k], z_send.at[way, 3 + k], z_recv.at[way, 3 + k],
-            device_id={"shard": target(way)}, device_id_type=ALONG)
+    half = tokens // 2
+
+    def s_move(way, k, h, who):
+        rows = pl.ds(half * h, half)
+        return pltpu.make_async_remote_copy(
+            tx.at[way, k, rows], rx.at[way, k, rows], z_send.at[way, GS + 2 * k + h], z_recv.at[way, GS + 2 * k + h],
+            device_id={"shard": who}, device_id_type=ALONG)
+
+    def s_copy(way, k, h):
+        return s_move(way, k, h, target(way))
 
     def g_copy(way, i):
         lo, hi = GSPANS[i]
@@ -252,7 +272,7 @@
     def _():
         out_way = jnp.where(z == 0, 1, 0)
         in_way = 1 - out_way
-        for i in range(3):
+        for i in range(GS):
             for n in range(*GSPANS[i]):
                 gtx[out_way, n] = gpart(n).astype(jnp.bfloat16)
             g_copy(out_way, i).start()
@@ -260,12 +280,13 @@
         def push(k, carry):
             t, j = k // own, lax.rem(k, own)
             tx[out_way, k] = contribution(owner_of(out_way, t), j).astype(jnp.bfloat16)
-            s_copy(out_way, k).start()
+            for h in range(2):
+                s_copy(out_way, k, h).start()
             return carry
 
         lax.fori_loop(0, pieces, push, 0)
 
-        for i in range(3):
+        for i in range(GS):
             lo, hi = GSPANS[i]
             pltpu.make_async_remote_copy(
                 gtx.at[in_way, lo:hi], grx.at[in_way, lo:hi], z_send.at[in_way, i], z_recv.at[in_way, i],
@@ -299,9 +320,8 @@
             for j in range(lo, hi):
                 k = own * t + j
                 mine = contribution(owner_of(in_way, t), j)
-                pltpu.make_async_remote_copy(
-                    tx.at[in_way, k], rx.at[in_way, k], z_send.at[in_way, 3 + k], z_recv.at[in_way, 3 + k],
-                    device_id={"shard": target(out_way)}, device_id_type=ALONG).wait_recv()
+                for h in range(2):
+                    s_move(in_way, k, h, target(out_way)).wait_recv()
                 done = (rx[in_way, k].astype(jnp.float32) + mine).astype(jnp.bfloat16)
                 sketch[t, :, width * j : width * (j + 1)] = done
             cols = sketch[t, :, width * lo : width * hi]
@@ -366,11 +386,12 @@
             p_copy(q).wait_send()
             for m in (1, 2, 3):
                 r_copy(q, m).wait_send()
-        for i in range(3):
+        for i in range(GS):
             g_copy(out_way, i).wait_send()
 
         def drain(k, carry):
-            s_copy(out_way, k).wait_send()
+            for h in range(2):
+                s_copy(out_way, k, h).wait_send()
             return carry
 
         lax.fori_loop(0, pieces, drain, 0)
@@ -389,17 +410,19 @@
         def pass_s(way, k):
             t, j = k // own, lax.rem(k, own)
             mine = contribution(owner_of(way, t), j)
-            s_copy(way, k).wait_recv()
-            tx[way, k] = (rx[way, k].astype(jnp.float32) + mine).astype(jnp.bfloat16)
-            s_copy(way, k).start()
-
-        pass_g(near, 0)
-        pass_g(near, 1)
-        pass_g(far, 0)
-        pass_g(near, 2)
-        pass_g(far, 1)
+            for h in range(2):
+                s_copy(way, k, h).wait_recv()
+                rows = slice(half * h, half * (h + 1))
+                tx[way, k, rows] = (rx[way, k, rows].astype(jnp.float32) + mine[rows]).astype(jnp.bfloat16)
+                s_copy(way, k, h).start()
+
+        for i in range(GS):
+            pass_g(near, i)
+            if i >= 2:
+                pass_g(far, i - 2)
         pass_s(near, 0)
-        pass_g(far, 2)
+        pass_g(far, GS - 2)
+        pass_g(far, GS - 1)
 
         def both_ways(k, carry):
             pass_s(near, k)
@@ -417,12 +440,13 @@
         for c in range(CHUNKS):
             settle(c)
         for way in range(2):
-            for i in range(3):
+            for i in range(GS):
                 g_copy(way, i).wait_send()
 
         def drain(k, carry):
-            s_copy(0, k).wait_send()
-            s_copy(1, k).wait_send()
+            for way in range(2):
+                for h in range(2):
+                    s_copy(way, k, h).wait_send()
             return carry
 
         lax.fori_loop(0, pieces, drain, 0)
@@ -430,16 +454,29 @@
     out[...] = gathered[...]
 
 
-def assemble_kernel(got, out):
-    for c, (lo, hi) in enumerate(SPANS):
-        for j in range(lo, hi):
-            for i in range(hi):
-                u = FIRST[c] + (j - lo) * hi + i
-                rows = [got[2 * n + h, u] for h in range(2) for n in range(4)]
-                unit = jnp.concatenate(rows, axis=0).astype(jnp.float32)
-                out[128 * i : 128 * (i + 1), 128 * j : 128 * (j + 1)] = unit
-                if i < lo:
-                    out[128 * j : 128 * (j + 1), 128 * i : 128 * (i + 1)] = unit.T
+def assemble_kernel(got, out, held, sems):
+    chunk_of = [c for c, (lo, hi) in enumerate(SPANS) for _ in range(lo, hi)]
+
+    def unit(i, j):
+        c = chunk_of[j]
+        lo, hi = SPANS[c]
+        u = FIRST[c] + (j - lo) * hi + i
+        rows = [got[2 * n + h, u] for h in range(2) for n in range(4)]
+        return jnp.concatenate(rows, axis=0).astype(jnp.float32)
+
+    count = len(chunk_of)
+
+    def put(i):
+        rows = pl.ds(BLK * i, BLK)
+        return pltpu.make_async_copy(held.at[rows], out.at[rows], sems.at[i])
+
+    for i in range(count):
+        for j in range(count):
+            block = unit(i, j) if i < SPANS[chunk_of[j]][1] else unit(j, i).T
+            held[BLK * i : BLK * (i + 1), BLK * j : BLK * (j + 1)] = block
+        put(i).start()
+    for i in range(count):
+        put(i).wait()
 
 
 def fast_body(shards, parts, activations, out_grads, sign_bits, block_ids):
@@ -450,11 +487,18 @@
     bf, f32 = jnp.bfloat16, jnp.float32
     dma = pltpu.SemaphoreType.DMA
     number = shards * own
+    hbm = pl.BlockSpec(memory_space=pltpu.HBM)
     picked = pl.pallas_call(
         functools.partial(pick_kernel, shards, own, per),
         out_shape=jax.ShapeDtypeStruct((number, tokens, BLK), bf),
-        in_specs=[pl.BlockSpec(memory_space=pltpu.SMEM), vmem, vmem],
+        in_specs=[hbm, hbm, hbm],
         out_specs=vmem,
+        scratch_shapes=[
+            pltpu.SMEM(block_ids.shape, jnp.int32),
+            pltpu.VMEM((columns,), jnp.int32),
+            pltpu.VMEM((4, tokens // 4, columns), bf),
+            dma((6,)),
+        ],
         compiler_params=pltpu.CompilerParams(vmem_limit_bytes=12 * 2**20),
         name="pick",
     )(block_ids, sign_bits, out_grads)
@@ -476,7 +520,7 @@
             pltpu.VMEM((4, 2 * UNITS, 16, BLK), bf),
             pltpu.VMEM((4, 2 * UNITS, 16, BLK), bf),
             pltpu.VMEM((parts, UNITS, 16, BLK), bf),
-            dma((2, 3 + 2 * own)), dma((2, 3 + 2 * own)),
+            dma((2, GS + 4 * own)), dma((2, GS + 4 * own)),
             dma((2 * CHUNKS,)), dma((2 * CHUNKS,)),
             dma((2 * CHUNKS, 3)), dma((2 * CHUNKS, 3)),
             dma((CHUNKS,)), dma((CHUNKS,)),
@@ -490,7 +534,8 @@
         assemble_kernel,
         out_shape=jax.ShapeDtypeStruct((own * BLK, own * BLK), f32),
         in_specs=[vmem],
-        out_specs=vmem,
+        out_specs=hbm,
+        scratch_shapes=[pltpu.VMEM((own * BLK, own * BLK), f32), dma((own,))],
         compiler_params=pltpu.CompilerParams(vmem_limit_bytes=16 * 2**20),
         name="assemble",
     )(got)

time: 92.9 us -> 91.7 us (0.987)
  Pallas kernels: 89.2 us -> 88 us
    pallas_call x1, Pallas kernels: 84.6 us -> 82.4 us  [fast_body(): pl.pallas_call(functools.partial(mix_kernel, shards, parts, own), out_sha...]
    pallas_call x1, Pallas kernels: 2.1 us -> 3.45 us  [fast_body(): pl.pallas_call(functools.partial(pick_kernel, shards, own, per), out_shap...]
where the time goes in v3:
time: 91.7 us; the launch traced here: 91.5 us
  Pallas kernels  88 us (96%)
  local copies, waits for them, and re-layouts  3.44 us (4%)
    pallas_call x1, Pallas kernels, fast_body(): pl.pallas_call(functools.partial(mix_kernel, shards, parts, own), out_sha...  82.4 us
    pallas_call x1, Pallas kernels, fast_body(): pl.pallas_call(functools.partial(pick_kernel, shards, own, per), out_shap...  3.45 us
    unnamed x8, local copies, waits for them, and re-layouts  3.44 us
    pallas_call x1, Pallas kernels, fast_body(): pl.pallas_call(assemble_kernel, out_shape=jax.ShapeDtypeStruct((own * BLK...  2.13 us

profile of v3, /device:TPU:0, one launch (start us, length us, event | category | flops | bytes accessed | tf_op | source)
XLA Modules:
  0.0 91.5 jit_solution(773216222575343723)
XLA Ops:
  0.0 0.0 copy-start
  0.0 2.0 %copy-done = bf16[512,3584]{1,0:T(8,128)(2,1)S(1)} copy-done((bf16[512,3584]{1,0:T(8,128)(2,1)S(1)}, bf16[512,3584]{1,0:T(8,128)(2,1)}, u32[]{:S(2)}) %copy-start) | copy-done | bytes 3670040
  2.0 0.0 copy-start.2
  2.0 0.7 copy-done.2
  2.8 0.0 copy-start.3
  2.8 0.7 copy-done.3
  3.4 0.0 copy-start.1
  3.4 3.5 %pick.1.picked = bf16[32,512,128]{2,1,0:T(8,128)(2,1)S(1)} custom-call(s32[4,8]{1,0:T(4,128)S(1)} %copy-done.3, s32[3584]{0:T(1024)S(1)} %copy-done.2, bf16[512,3584]{1,0:T(8,128)(2,1)S(1)} %copy-done), custom_call_target="tpu_custom_call" | custom-call | tf_op jit(solution)/shard_map/pick/pallas_call | solution.py:491
  6.9 0.0 copy-done.1
  6.9 82.4 %mix.1.got = bf16[8,39,16,128]{3,2,1,0:T(8,128)(2,1)S(1)} custom-call(bf16[512,1024]{1,0:T(8,128)(2,1)S(1)} %copy-done.1, bf16[32,512,128]{2,1,0:T(8,128)(2,1)S(1)} %pick.1.picked), custom_call_target="tpu_custom_call" | custom-call | tf_op jit(solution)/shard_map/mix/pallas_call | solution.py:505
  89.4 2.1 %assemble.1 = f32[1024,1024]{1,0:T(8,128)} custom-call(bf16[8,39,16,128]{3,2,1,0:T(8,128)(2,1)S(1)} %mix.1.got), custom_call_target="tpu_custom_call" | custom-call | tf_op jit(solution)/shard_map/assemble/pallas_call | solution.py:533
Async XLA Ops:
  0.0 2.0 %copy-start = (bf16[512,3584]{1,0:T(8,128)(2,1)S(1)}, bf16[512,3584]{1,0:T(8,128)(2,1)}, u32[]{:S(2)}) copy-start(bf16[512,3584]{1,0:T(8,128)(2,1)} %grads.1) | copy-start | bytes 11010052
  2.0 0.7 copy-start.2
  2.8 0.7 copy-start.3
  3.4 3.5 %copy-start.1 = (bf16[512,1024]{1,0:T(8,128)(2,1)S(1)}, bf16[512,1024]{1,0:T(8,128)(2,1)}, u32[]{:S(2)}) copy-start(bf16[512,1024]{1,0:T(8,128)(2,1)} %act.1) | copy-start | bytes 3145732

commit v4 on v3

--- a/solution.py
+++ b/solution.py
@@ -83,43 +83,31 @@
 TRIANGLE = tuple((i, j) for i in range(4) for j in range(i + 1))
 GSPANS = ((0, 2), (2, 4), (4, 6), (6, 8), (8, 10))
 GS = len(GSPANS)
-
-
-def pick_kernel(shards, own, per, ids_in, bits_in, grads, out, ids, bits, held, sems):
+CUTS = 4
+
+
+def pick_kernel(shards, own, per, ids, bits, grads, out):
     z = lax.axis_index("shard")
     width = BLK
     number = shards * own
-    cuts = held.shape[0]
-    rows = held.shape[1]
-
-    def fetch(n):
-        return pltpu.make_async_copy(grads.at[pl.ds(rows * n, rows)], held.at[n], sems.at[n])
-
-    early = (pltpu.make_async_copy(ids_in, ids, sems.at[cuts]), pltpu.make_async_copy(bits_in, bits, sems.at[cuts + 1]))
-    for copy in early:
-        copy.start()
-    for n in range(cuts):
-        fetch(n).start()
-    for copy in early:
-        copy.wait()
-    for n in range(cuts):
-        fetch(n).wait()
-
-        def take(p, carry):
-            block = ids[p // own, lax.rem(p, own)]
-            r = block // per
-            start = pl.multiple_of((block - r * per) * width, width)
-            common = r & z
-            odd = common & 1
-            for level in range(1, shards.bit_length() - 1):
-                odd = odd + ((common >> level) & 1)
-            sign = 1 - 2 * (odd & 1)
-            flips = (1 - 2 * bits[pl.ds(start, width)].reshape(1, width)) * sign
-            flips = flips.astype(jnp.float32).astype(jnp.bfloat16)
-            out[p, rows * n : rows * (n + 1)] = held[n, :, pl.ds(start, width)] * flips
-            return carry
-
-        lax.fori_loop(0, number, take, 0, unroll=4)
+
+    def start_of(p):
+        block = ids[p // own, lax.rem(p, own)]
+        r = block // per
+        return r, pl.multiple_of((block - r * per) * width, width)
+
+    def take(p, carry):
+        r, start = start_of(p)
+        common = r & z
+        odd = common & 1
+        for level in range(1, shards.bit_length() - 1):
+            odd = odd + ((common >> level) & 1)
+        sign = 1 - 2 * (odd & 1)
+        signs = ((1 - 2 * bits[pl.ds(start, width)].reshape(1, width)) * sign).astype(jnp.float32).astype(jnp.bfloat16)
+        out[p] = grads[:, pl.ds(start, width)] * signs
+        return carry
+
+    lax.fori_loop(0, number, take, 0, unroll=4)
 
 
 def mix_kernel(
@@ -178,12 +166,12 @@
     def target(way):
         return jnp.where(way == 0, z - 1, z + 1)
 
-    half = tokens // 2
+    half = tokens // CUTS
 
     def s_move(way, k, h, who):
         rows = pl.ds(half * h, half)
         return pltpu.make_async_remote_copy(
-            tx.at[way, k, rows], rx.at[way, k, rows], z_send.at[way, GS + 2 * k + h], z_recv.at[way, GS + 2 * k + h],
+            tx.at[way, k, rows], rx.at[way, k, rows], z_send.at[way, GS + CUTS * k + h], z_recv.at[way, GS + CUTS * k + h],
             device_id={"shard": who}, device_id_type=ALONG)
 
     def s_copy(way, k, h):
@@ -280,7 +268,7 @@
         def push(k, carry):
             t, j = k // own, lax.rem(k, own)
             tx[out_way, k] = contribution(owner_of(out_way, t), j).astype(jnp.bfloat16)
-            for h in range(2):
+            for h in range(CUTS):
                 s_copy(out_way, k, h).start()
             return carry
 
@@ -320,7 +308,7 @@
             for j in range(lo, hi):
                 k = own * t + j
                 mine = contribution(owner_of(in_way, t), j)
-                for h in range(2):
+                for h in range(CUTS):
                     s_move(in_way, k, h, target(out_way)).wait_recv()
                 done = (rx[in_way, k].astype(jnp.float32) + mine).astype(jnp.bfloat16)
                 sketch[t, :, width * j : width * (j + 1)] = done
@@ -390,7 +378,7 @@
             g_copy(out_way, i).wait_send()
 
         def drain(k, carry):
-            for h in range(2):
+            for h in range(CUTS):
                 s_copy(out_way, k, h).wait_send()
             return carry
 
@@ -410,7 +398,7 @@
         def pass_s(way, k):
             t, j = k // own, lax.rem(k, own)
             mine = contribution(owner_of(way, t), j)
-            for h in range(2):
+            for h in range(CUTS):
                 s_copy(way, k, h).wait_recv()
                 rows = slice(half * h, half * (h + 1))
                 tx[way, k, rows] = (rx[way, k, rows].astype(jnp.float32) + mine[rows]).astype(jnp.bfloat16)
@@ -445,7 +433,7 @@
 
         def drain(k, carry):
             for way in range(2):
-                for h in range(2):
+                for h in range(CUTS):
                     s_copy(way, k, h).wait_send()
             return carry
 
@@ -491,14 +479,8 @@
     picked = pl.pallas_call(
         functools.partial(pick_kernel, shards, own, per),
         out_shape=jax.ShapeDtypeStruct((number, tokens, BLK), bf),
-        in_specs=[hbm, hbm, hbm],
+        in_specs=[pl.BlockSpec(memory_space=pltpu.SMEM), vmem, vmem],
         out_specs=vmem,
-        scratch_shapes=[
-            pltpu.SMEM(block_ids.shape, jnp.int32),
-            pltpu.VMEM((columns,), jnp.int32),
-            pltpu.VMEM((4, tokens // 4, columns), bf),
-            dma((6,)),
-        ],
         compiler_params=pltpu.CompilerParams(vmem_limit_bytes=12 * 2**20),
         name="pick",
     )(block_ids, sign_bits, out_grads)
@@ -520,7 +502,7 @@
             pltpu.VMEM((4, 2 * UNITS, 16, BLK), bf),
             pltpu.VMEM((4, 2 * UNITS, 16, BLK), bf),
             pltpu.VMEM((parts, UNITS, 16, BLK), bf),
-            dma((2, GS + 4 * own)), dma((2, GS + 4 * own)),
+            dma((2, GS + 2 * CUTS * own)), dma((2, GS + 2 * CUTS * own)),
             dma((2 * CHUNKS,)), dma((2 * CHUNKS,)),
             dma((2 * CHUNKS, 3)), dma((2 * CHUNKS, 3)),
             dma((CHUNKS,)), dma((CHUNKS,)),

time: 91.7 us -> 91.5 us (level)
    pallas_call x1, Pallas kernels: 3.45 us -> 1.46 us  [fast_body(): pl.pallas_call(functools.partial(pick_kernel, shards, own, per), out_shap...]
    pallas_call x1, Pallas kernels: 82.4 us -> 84.2 us  [fast_body(): pl.pallas_call(functools.partial(mix_kernel, shards, parts, own), out_sha...]
where the time goes in v4:
time: 91.5 us; the launch traced here: 91.2 us
  Pallas kernels  87.8 us (96%)
  local copies, waits for them, and re-layouts  3.44 us (4%)
    pallas_call x1, Pallas kernels, fast_body(): pl.pallas_call(functools.partial(mix_kernel, shards, parts, own), out_sha...  84.2 us
    unnamed x8, local copies, waits for them, and re-layouts  3.44 us
    pallas_call x1, Pallas kernels, fast_body(): pl.pallas_call(assemble_kernel, out_shape=jax.ShapeDtypeStruct((own * BLK...  2.13 us

profile of v4, /device:TPU:0, one launch (start us, length us, event | category | flops | bytes accessed | tf_op | source)
XLA Modules:
  0.0 91.2 jit_solution(303508766631036425)
XLA Ops:
  0.0 0.0 copy-start
  0.0 2.0 %copy-done = bf16[512,3584]{1,0:T(8,128)(2,1)S(1)} copy-done((bf16[512,3584]{1,0:T(8,128)(2,1)S(1)}, bf16[512,3584]{1,0:T(8,128)(2,1)}, u32[]{:S(2)}) %copy-start) | copy-done | bytes 3670040
  2.0 0.0 copy-start.2
  2.0 0.7 copy-done.2
  2.8 0.0 copy-start.3
  2.8 0.7 copy-done.3
  3.4 0.0 copy-start.1
  3.4 1.5 %pick.1.picked = bf16[32,512,128]{2,1,0:T(8,128)(2,1)S(1)} custom-call(s32[4,8]{1,0:T(4,128)S(1)} %copy-done.3, s32[3584]{0:T(1024)S(1)} %copy-done.2, bf16[512,3584]{1,0:T(8,128)(2,1)S(1)} %copy-done), custom_call_target="tpu_custom_call" | custom-call | tf_op jit(solution)/shard_map/pick/pallas_call | solution.py:479
  4.9 0.0 copy-done.1
  4.9 84.2 %mix.1.got = bf16[8,39,16,128]{3,2,1,0:T(8,128)(2,1)S(1)} custom-call(bf16[512,1024]{1,0:T(8,128)(2,1)S(1)} %copy-done.1, bf16[32,512,128]{2,1,0:T(8,128)(2,1)S(1)} %pick.1.picked), custom_call_target="tpu_custom_call" | custom-call | tf_op jit(solution)/shard_map/mix/pallas_call | solution.py:487
  89.1 2.1 %assemble.1 = f32[1024,1024]{1,0:T(8,128)} custom-call(bf16[8,39,16,128]{3,2,1,0:T(8,128)(2,1)S(1)} %mix.1.got), custom_call_target="tpu_custom_call" | custom-call | tf_op jit(solution)/shard_map/assemble/pallas_call | solution.py:515
Async XLA Ops:
  0.0 2.0 %copy-start = (bf16[512,3584]{1,0:T(8,128)(2,1)S(1)}, bf16[512,3584]{1,0:T(8,128)(2,1)}, u32[]{:S(2)}) copy-start(bf16[512,3584]{1,0:T(8,128)(2,1)} %grads.1) | copy-start | bytes 11010052
  2.0 0.7 copy-start.2
  2.8 0.7 copy-start.3
  3.4 1.5 %copy-start.1 = (bf16[512,1024]{1,0:T(8,128)(2,1)S(1)}, bf16[512,1024]{1,0:T(8,128)(2,1)}, u32[]{:S(2)}) copy-start(bf16[512,1024]{1,0:T(8,128)(2,1)} %act.1) | copy-start | bytes 3145732
